TPU v7x, 256 devices: a whole 4x4x8 slice. The times are simulated.
256 devices in a mesh: dp: 8 (over z), own: 32 (over x, y, core).
Axes of the slice: x: 4, y: 4, z: 8, core: 2. Of those that a mesh axis runs over, the one named last changes fastest.
Arguments:
- signals: bfloat16 [65536, 384], P(('dp', 'own')), may hold values from -6 to 6
- cotangent: bfloat16 [65536, 384], P(('dp', 'own')), may hold values from -6 to 6
- row_insertion: int32 [65536], P(('dp', 'own')), may hold values from 0 to 63, as said below
- touched: int32 [256, 4], replicated, may hold values from 0 to 63, as said below
- slot_map: int32 [64], replicated, may hold values from 0 to 63, each once
- weights: bfloat16 [64, 2, 384, 1024], P(None, None, 'own'), may hold values from -0.3125 to 0.3125
- moment1: float32 [64, 2, 384, 1024], P(None, None, 'own', 'dp'), may hold values from -25.6 to 25.6
- moment2: float32 [64, 2, 384, 1024], P(None, None, 'own', 'dp'), may hold values from 0.2048 to 6.144
Outputs:
- predicted: bfloat16 [65536, 384], P(('dp', 'own'))
- new_weights: bfloat16 [64, 2, 384, 1024], P(None, None, 'own')
- new_moment1: float32 [64, 2, 384, 1024], P(None, None, 'own', 'dp')
- new_moment2: float32 [64, 2, 384, 1024], P(None, None, 'own', 'dp')
Inputs may be any that keep to these rules, and one draw needn't show every extreme that they name: `row_insertion`: device d (dp index times the size of own plus own index) holds rows d * 256 to (d + 1) * 256 - 1; their insertions are all in row d of touched; at most 128 rows of one device name the same insertion, and on every device one insertion is named by exactly 128 rows. `touched`: each row lists 4 different insertions.
All inputs are finite; a program needn't handle non-finite values.
Results may differ from a plain program's by a relative error of at most 0.0049.
Values may be sent and summed in bfloat16 or wider, within the bound.
A program may use at most 128 MiB of HBM per device.

v0:
```python
import math
import jax
import jax.numpy as jnp
from jax import lax
from jax.sharding import PartitionSpec as P

SITES = 384
WIDTH = 1024
TOUCH = 4
CAP = 128
gelu_coef = math.sqrt(2.0 / math.pi)
cubic_coef = 0.044715
learn_rate = 0.01
highest = lax.Precision.HIGHEST


def gelu_parts(preact):
    tanh_input = gelu_coef * (preact + cubic_coef * preact * preact * preact)
    tangent = jnp.tanh(tanh_input)
    gelu_val = 0.5 * preact * (1.0 + tangent)
    slopes = 0.5 * (1.0 + tangent) + 0.5 * preact * (1.0 - tangent * tangent) * gelu_coef * (
        1.0 + 3.0 * cubic_coef * preact * preact
    )
    return (gelu_val, slopes)


def dispatch(row_ids, listed):
    match_table = (row_ids[:, None] == listed[None, :]).astype(jnp.int32)
    running = jnp.cumsum(match_table, axis=0) - 1
    slot_of = jnp.sum(match_table * jnp.arange(listed.shape[0], dtype=jnp.int32)[None, :], axis=1)
    within = jnp.sum(match_table * running, axis=1)
    return slot_of * CAP + within


def adam_step(params, moment_one, moment_two, gradient):
    moment_one = 0.9 * moment_one + 0.1 * gradient
    moment_two = 0.999 * moment_two + 0.001 * gradient * gradient
    correct_one = 1.0 - 0.9**10
    correct_two = 1.0 - 0.999**10
    updated = params - learn_rate * (moment_one / correct_one) / (
        jnp.sqrt(moment_two / correct_two) + 1e-08
    )
    return (updated.astype(jnp.bfloat16), moment_one, moment_two)


def sum_by_insertion(item_rows, arrived_grad, number):
    one_hot = (jnp.arange(number, dtype=jnp.int32)[:, None] == item_rows[None, :]).astype(
        arrived_grad.dtype
    )
    flat_grad = arrived_grad.reshape(item_rows.shape[0], -1)
    return jnp.dot(one_hot, flat_grad, preferred_element_type=jnp.float32)


def shards(signals, cotangent, row_insertion, touched, slot_map, weights, moment1, moment2):
    n_own = lax.axis_size("own")
    n_dp = lax.axis_size("dp")
    dp_at = lax.axis_index("dp")
    own_at = lax.axis_index("own")
    number = weights.shape[0]
    piece_rows = weights.shape[2]
    width_part = moment1.shape[3]
    stored = jnp.sum(
        jnp.where(
            touched[:, :, None] == jnp.arange(number, dtype=jnp.int32)[None, None, :],
            slot_map[None, None, :],
            0,
        ),
        axis=2,
    )
    stored_all = stored.reshape(n_dp, n_own, TOUCH)
    group_rows = lax.dynamic_index_in_dim(stored_all, dp_at, 0, keepdims=False)
    flat_rows = group_rows.reshape(-1)
    my_list = lax.dynamic_index_in_dim(touched, dp_at * n_own + own_at, 0, keepdims=False)
    places = dispatch(row_insertion, my_list)
    stacked = (
        jnp.zeros((TOUCH * CAP, 2 * SITES), signals.dtype)
        .at[places]
        .set(jnp.concatenate([signals, cotangent], axis=1))
    )
    stacked = stacked.reshape(TOUCH, CAP, 2 * SITES)
    sig_slots = stacked[:, :, :SITES]
    cot_slots = stacked[:, :, SITES:]
    read_out = None
    outgoing = jnp.take(weights, flat_rows, axis=0).reshape(n_own, TOUCH, 2, piece_rows, WIDTH)
    arrived = lax.all_to_all(outgoing, "own", split_axis=0, concat_axis=3, tiled=True)
    read_in = arrived[0, :, 0]
    read_out = arrived[0, :, 1]
    preact = jnp.einsum("kcs,ksw->kcw", sig_slots, read_in, preferred_element_type=jnp.float32)
    gelu_val, slopes = gelu_parts(preact)
    hidden = gelu_val.astype(jnp.bfloat16)
    pred_slots = jnp.einsum(
        "kcw,ksw->kcs", hidden, read_out, preferred_element_type=jnp.float32
    ).astype(jnp.bfloat16)
    back_hidden = jnp.einsum(
        "kcs,ksw->kcw", cot_slots, read_out, preferred_element_type=jnp.float32
    )
    back_pre = (back_hidden * slopes).astype(jnp.bfloat16)
    grad_in = jnp.einsum("kcs,kcw->ksw", sig_slots, back_pre, preferred_element_type=jnp.float32)
    grad_out = jnp.einsum("kcs,kcw->ksw", cot_slots, hidden, preferred_element_type=jnp.float32)
    grads = jnp.stack([grad_in, grad_out], axis=1).astype(jnp.bfloat16)
    pieces = grads.reshape(TOUCH, 2, n_own, piece_rows, n_dp, width_part)
    pieces = pieces.transpose(4, 2, 0, 1, 3, 5).reshape(
        n_dp * n_own, TOUCH, 2, piece_rows, width_part
    )
    arrived_grad = lax.all_to_all(pieces, ("dp", "own"), split_axis=0, concat_axis=0, tiled=True)
    table = sum_by_insertion(stored.reshape(-1), arrived_grad, number).reshape(
        number, 2, piece_rows, width_part
    )
    own_params = lax.dynamic_slice_in_dim(weights, dp_at * width_part, width_part, 3).astype(
        jnp.float32
    )
    fresh_part, new_moment1, new_moment2 = adam_step(own_params, moment1, moment2, table)
    new_weights = lax.all_gather(fresh_part, "dp", axis=3, tiled=True)
    predicted = pred_slots.reshape(TOUCH * CAP, SITES)[places]
    return (predicted, new_weights, new_moment1, new_moment2)


def solution(mesh):
    in_specs = (
        P(("dp", "own"), None),
        P(("dp", "own"), None),
        P(("dp", "own")),
        P(),
        P(),
        P(None, None, "own", None),
        P(None, None, "own", "dp"),
        P(None, None, "own", "dp"),
    )
    out_specs = (
        P(("dp", "own"), None),
        P(None, None, "own", None),
        P(None, None, "own", "dp"),
        P(None, None, "own", "dp"),
    )
    return jax.shard_map(shards, mesh=mesh, in_specs=in_specs, out_specs=out_specs, check_vma=False)
```

profile of v0, /device:TPU:32, one launch (start us, length us, event | category | flops | bytes accessed | tf_op | source)
XLA Modules:
  0.0 435.3 jit_solution(7643077568396394921)
XLA Ops:
  9.1 16.2 %gather_fusion = bf16[128,2,12,1024]{3,1,2,0:T(2,128)(2,1)} fusion(bf16[64,2,12,1024]{3,1,2,0:T(2,128)(2,1)S(1)} %copy-done, s32[1024]{0:T(1024)S(1)} %pad_clamp_fusion.1), kind=kCustom, calls=%fused_computation | custom fusion | bytes 12583424 | tf_op jit(solution)/shard_map/jit(_take)/gather | solution.py:84
  25.3 8.9 %broadcast_select_fusion = bf16[32,4,2,12,1024]{4,2,3,1,0:T(2,128)(2,1)} fusion(bf16[32,4,2,12,1024]{4,2,3,1,0:T(2,128)(2,1)} %bitcast.60, pred[32,4]{1,0:T(8,128)(4,1)S(1)} %copy.89), kind=kLoop, calls=%fused_computation.3 | loop fusion | flops 3145728 | bytes 12583040 | tf_op jit(solution)/shard_map/jit(_take)/select_n | solution.py:84
  34.2 7.6 %all-to-all-start = ((bf16[32,4,2,12,1024]{4,2,3,1,0:T(2,128)(2,1)}), bf16[32,4,2,12,1024]{4,2,3,1,0:T(2,128)(2,1)}, u32[]{:S(2)}, u32[]{:S(2)}) async-start(bf16[32,4,2,12,1024]{4,2,3,1,0:T(2,128)(2,1)} %broadcast_select_fusion), calls=%async_computation | async-start | bytes 12582912 | tf_op jit(solution)/shard_map/all_to_all | solution.py:85
  43.8 3.0 scatter_custom_fusion
  46.8 74.9 %all-to-all-done = bf16[32,4,2,12,1024]{4,2,3,1,0:T(2,128)(2,1)} async-done(((bf16[32,4,2,12,1024]{4,2,3,1,0:T(2,128)(2,1)}), bf16[32,4,2,12,1024]{4,2,3,1,0:T(2,128)(2,1)}, u32[]{:S(2)}, u32[]{:S(2)}) %all-to-all-start) | async-done | bytes 6291488 | tf_op jit(solution)/shard_map/all_to_all | solution.py:85
  121.7 6.4 %copy.90 = bf16[1,4,2,32,12,1024]{5,2,4,3,1,0:T(2,128)(2,1)S(1)} copy(bf16[1,4,2,32,12,1024]{5,2,4,1,3,0:T(2,128)(2,1)} %bitcast.11) | data formatting | bytes 12582912 | tf_op jit(solution)/shard_map/all_to_all | solution.py:85
  128.1 10.3 %fusion.40 = (bf16[1,4,1,384,1024]{4,2,3,1,0:T(2,128)(2,1)S(1)}, bf16[1,4,1,384,1024]{4,2,3,1,0:T(2,128)(2,1)}) fusion(bf16[1,4,2,384,1024]{4,2,3,1,0:T(2,128)(2,1)S(1)} %bitcast.59), kind=kLoop, calls=%fused_computation.70 | loop fusion | bytes 12582912 | tf_op jit(solution)/shard_map/slice | solution.py:86
  141.7 2.9 copy.99
  144.6 8.4 %convolution_convert_fusion.1 = bf16[4,384,1024]{2,1,0:T(8,128)(2,1)} fusion(f32[4,128,1024]{2,1,0:T(8,128)} %copy-done.3, bf16[1,4,1,384,1024]{4,2,3,1,0:T(2,128)(2,1)} %get-tuple-element.30, bf16[4,128,768]{2,1,0:T(8,128)(2,1)} %bitcast.69), kind=kOutput, calls=%fused_computation.11 | convolution fusion | flops 816840704 | bytes 9175040 | tf_op jit(solution)/shard_map/kcs,kcw->ksw/dot_general | solution.py:98
  153.0 2.7 copy.115
  157.6 3.1 pad_maximum_fusion
  160.7 10.5 %copy.100 = bf16[256,4,2,12,128]{4,1,3,2,0:T(4,128)(2,1)} copy(bf16[256,4,2,12,128]{4,0,3,2,1:T(8,128)(2,1)} %bitcast.62) | data formatting | bytes 12582912 | tf_op jit(solution)/shard_map/reshape | solution.py:102
  171.2 20.5 %all-to-all-start.1 = ((bf16[256,4,2,12,128]{4,1,3,2,0:T(4,128)(2,1)}), bf16[256,4,2,12,128]{4,1,3,2,0:T(4,128)(2,1)}, u32[]{:S(2)}, u32[]{:S(2)}) async-start(bf16[256,4,2,12,128]{4,1,3,2,0:T(4,128)(2,1)} %copy.100), calls=%async_computation.1 | async-start | bytes 12582912 | tf_op jit(solution)/shard_map/all_to_all | solution.py:105
  192.2 141.6 %all-to-all-done.1 = bf16[256,4,2,12,128]{4,1,3,2,0:T(4,128)(2,1)} async-done(((bf16[256,4,2,12,128]{4,1,3,2,0:T(4,128)(2,1)}), bf16[256,4,2,12,128]{4,1,3,2,0:T(4,128)(2,1)}, u32[]{:S(2)}, u32[]{:S(2)}) %all-to-all-start.1) | async-done | bytes 6291488 | tf_op jit(solution)/shard_map/all_to_all | solution.py:105
  333.8 8.7 %copy.101 = bf16[256,4,2,12,128]{4,3,2,1,0:T(8,128)(2,1)} copy(bf16[256,4,2,12,128]{4,1,3,2,0:T(4,128)(2,1)} %all-to-all-done.1) | data formatting | bytes 12582912 | tf_op jit(solution)/shard_map/all_to_all | solution.py:105
  342.5 12.3 %reshape.132 = bf16[1024,3072]{1,0:T(8,128)(2,1)} reshape(bf16[256,4,2,12,128]{4,3,2,1,0:T(8,128)(2,1)} %copy.101) | data formatting | bytes 12582912 | tf_op jit(solution)/shard_map/reshape | solution.py:50
  354.7 8.7 %copy.102 = bf16[3072,1024]{1,0:T(8,128)(2,1)} copy(bf16[3072,1024]{0,1:T(8,128)(2,1)} %bitcast.63) | data formatting | bytes 12582912 | tf_op jit(solution)/shard_map/dot_general | solution.py:51
  363.4 7.0 %subtract_convert_fusion = (bf16[64,2,12,128]{3,0,2,1:T(8,128)(2,1)}, f32[64,2,12,128]{3,0,2,1:T(8,128)}, f32[64,2,12,128]{3,0,2,1:T(8,128)}) fusion(bf16[64,2,12,128]{3,1,2,0:T(2,128)(2,1)S(1)} %constant_dynamic-slice_fusion.1, f32[64,2,12,128]{3,1,2,0:T(2,128)} %param.14, f32[64,2,12,128]{3,1,2,0:T(2,128)} %param.15, ...), kind=kOutput, calls=%fused_computation.31 | convolution fusion | flops 405471232 | bytes 10227712 | tf_op jit(solution)/shard_map/dot_general | solution.py:51
  370.5 4.9 %convolution_convert_fusion.2 = bf16[4,128,384]{2,1,0:T(8,128)(2,1)S(1)} fusion(bf16[1,4,1,384,1024]{4,2,3,1,0:T(2,128)(2,1)} %get-tuple-element.30, f32[4,128,1024]{2,1,0:T(8,128)} %copy-done.3), kind=kOutput, calls=%fused_computation.20 | convolution fusion | flops 407568384 | bytes 5636096 | tf_op jit(solution)/shard_map/kcw,ksw->kcs/dot_general | solution.py:91
  375.4 1.8 gather_fusion.1
  377.2 2.7 copy.105
  379.9 1.5 copy.106
  381.4 40.0 %all-gather.2.cloned.1.call-done = bf16[64,2,12,1024]{3,0,2,1:T(8,128)(2,1)} async-done(((bf16[64,2,12,128]{3,0,2,1:T(8,128)(2,1)}), bf16[64,2,12,1024]{3,0,2,1:T(8,128)(2,1)}) %all-gather.2.cloned.1.call-update) | async-done | bytes 3145744 | tf_op jit(solution)/shard_map/all_gather | solution.py:113
  421.4 6.8 %copy.104 = bf16[64,2,12,1024]{3,1,2,0:T(2,128)(2,1)} copy(bf16[64,2,12,1024]{3,0,2,1:T(8,128)(2,1)} %all-gather.2.cloned.1.call-done) | data formatting | bytes 6291456
  (46 shorter events, 9.6 us)
Async XLA Ops:
  7.2 1.9 copy-start
  34.2 7.6 %copy-start.6 = (s32[256,4]{0,1:T(4,128)S(1)}, s32[256,4]{0,1:T(4,128)}, u32[]{:S(2)}) copy-start(s32[256,4]{0,1:T(4,128)} %param.11) | copy-start | bytes 12292
  34.2 7.8 %copy-start.7 = (s32[256]{0:T(256)S(1)}, s32[256]{0:T(256)}, u32[]{:S(2)}) copy-start(s32[256]{0:T(256)} %param.10) | copy-start | bytes 3076
  34.2 9.6 %copy-start.5 = (bf16[256,384]{1,0:T(8,128)(2,1)S(1)}, bf16[256,384]{1,0:T(8,128)(2,1)}, u32[]{:S(2)}) copy-start(bf16[256,384]{1,0:T(8,128)(2,1)} %param.9) | copy-start | bytes 589828
  34.2 87.4 %all-to-all-start = ((bf16[32,4,2,12,1024]{4,2,3,1,0:T(2,128)(2,1)}), bf16[32,4,2,12,1024]{4,2,3,1,0:T(2,128)(2,1)}, u32[]{:S(2)}, u32[]{:S(2)}) async-start(bf16[32,4,2,12,1024]{4,2,3,1,0:T(2,128)(2,1)} %broadcast_select_fusion), calls=%async_computation | async-start | bytes 12582912 | tf_op jit(solution)/shard_map/all_to_all | solution.py:85
  128.1 10.3 %copy-start.4 = (bf16[512,768]{1,0:T(8,128)(2,1)S(1)}, bf16[512,768]{1,0:T(8,128)(2,1)}, u32[]{:S(2)}) copy-start(bf16[512,768]{1,0:T(8,128)(2,1)} %scatter_custom_fusion) | copy-start | bytes 2359300
  139.6 1.3 copy-start.3
  155.7 1.9 copy-start.1
  171.2 162.7 %all-to-all-start.1 = ((bf16[256,4,2,12,128]{4,1,3,2,0:T(4,128)(2,1)}), bf16[256,4,2,12,128]{4,1,3,2,0:T(4,128)(2,1)}, u32[]{:S(2)}, u32[]{:S(2)}) async-start(bf16[256,4,2,12,128]{4,1,3,2,0:T(4,128)(2,1)} %copy.100), calls=%async_computation.1 | async-start | bytes 12582912 | tf_op jit(solution)/shard_map/all_to_all | solution.py:105
  191.7 229.7 %all-gather.2.cloned.1.call-start = ((), (), s32[]{:S(2)}) async-start(), calls=%async_computation.2 | async-start | bytes 3538944 | tf_op jit(solution)/shard_map/all_gather | solution.py:113
  377.2 2.7 copy-start.2
Sparse Core Ops, SparseCore 0:
  370.6 50.8 all-gather.1
where the time goes:
time: 442 us; the launch traced here: 435 us
  waiting for transfers between devices  257 us (58%)
  local copies, waits for them, and re-layouts  96.1 us (22%)
  starting transfers between devices  28.1 us (6%)
  matrix products  22.6 us (5%)
  other arithmetic  17.5 us (4%)
  between operations  14.5 us (3%)
    all_to_all x1, waiting for transfers between devices, shards(): lax.all_to_all(pieces, ('dp', 'own'), split_axis=0, concat_axis=0, tiled=...  142 us
    all_to_all x1, waiting for transfers between devices, shards(): lax.all_to_all(outgoing, 'own', split_axis=0, concat_axis=3, tiled=True)  74.9 us
    all_gather x1, waiting for transfers between devices, shards(): new_weights = lax.all_gather(fresh_part, 'dp', axis=3, tiled=True)  40 us
    all_to_all x1, starting transfers between devices, shards(): lax.all_to_all(pieces, ('dp', 'own'), split_axis=0, concat_axis=0, tiled=...  20.5 us
    gather x1, local copies, waits for them, and re-layouts, shards(): jnp.take(weights, flat_rows, axis=0)  16.2 us
    unnamed x21, local copies, waits for them, and re-layouts  15.9 us
    reshape x1, local copies, waits for them, and re-layouts, sum_by_insertion(): flat_grad = arrived_grad.reshape(item_rows.shape[0], -1)  12.3 us
    reshape x1, local copies, waits for them, and re-layouts, shards(): pieces.transpose(4, 2, 0, 1, 3, 5)  10.5 us
  transfers between devices with their start and end apart: 3, of which 3 were waited for; matrix products, arithmetic and copies ran while one was open for 4% of the time, Pallas kernels for 0%

commit v1 on v0

--- a/solution.py
+++ b/solution.py
@@ -110,7 +110,9 @@
         jnp.float32
     )
     fresh_part, new_moment1, new_moment2 = adam_step(own_params, moment1, moment2, table)
-    new_weights = lax.all_gather(fresh_part, "dp", axis=3, tiled=True)
+    new_weights = jnp.concatenate(
+        lax.all_to_all(jnp.stack([fresh_part] * lax.axis_size("dp")), "dp", 0, 0), axis=3
+    )
     predicted = pred_slots.reshape(TOUCH * CAP, SITES)[places]
     return (predicted, new_weights, new_moment1, new_moment2)
 

time: 442 us -> 460 us (1.041)
  waiting for transfers between devices: 257 us -> 277 us
  between operations: 14.5 us -> 1.1 us
  local copies, waits for them, and re-layouts: 96.1 us -> 101 us
  starting transfers between devices: 28.1 us -> 32.7 us
    all_to_all x0 -> x1, waiting for transfers between devices: none -> 60.5 us  [shards(): lax.all_to_all(jnp.stack([fresh_part] * lax.axis_size('dp')), 'dp', 0, 0)]
    all_gather x1 -> x0, waiting for transfers between devices: 40 us -> none  [shards(): new_weights = lax.all_gather(fresh_part, 'dp', axis=3, tiled=True)]
    all_to_all x0 -> x1, starting transfers between devices: none -> 4.61 us  [shards(): lax.all_to_all(jnp.stack([fresh_part] * lax.axis_size('dp')), 'dp', 0, 0)]
    unnamed x21 -> x19, local copies, waits for them, and re-layouts: 15.9 us -> 16.9 us
where the time goes in v1:
time: 460 us; the launch traced here: 451 us
  waiting for transfers between devices  277 us (60%)
  local copies, waits for them, and re-layouts  101 us (22%)
  starting transfers between devices  32.7 us (7%)
  matrix products  22.4 us (5%)
  other arithmetic  17.5 us (4%)
    all_to_all x1, waiting for transfers between devices, shards(): lax.all_to_all(pieces, ('dp', 'own'), split_axis=0, concat_axis=0, tiled=...  142 us
    all_to_all x1, waiting for transfers between devices, shards(): lax.all_to_all(outgoing, 'own', split_axis=0, concat_axis=3, tiled=True)  74.9 us
    all_to_all x1, waiting for transfers between devices, shards(): lax.all_to_all(jnp.stack([fresh_part] * lax.axis_size('dp')), 'dp', 0, 0)  60.5 us
    all_to_all x1, starting transfers between devices, shards(): lax.all_to_all(pieces, ('dp', 'own'), split_axis=0, concat_axis=0, tiled=...  20.5 us
    unnamed x19, local copies, waits for them, and re-layouts  16.9 us
    gather x1, local copies, waits for them, and re-layouts, shards(): jnp.take(weights, flat_rows, axis=0)  16.2 us
    reshape x1, local copies, waits for them, and re-layouts, sum_by_insertion(): flat_grad = arrived_grad.reshape(item_rows.shape[0], -1)  12.1 us
    reshape x1, local copies, waits for them, and re-layouts, shards(): pieces.transpose(4, 2, 0, 1, 3, 5)  10.5 us
  transfers between devices with their start and end apart: 3, of which 3 were waited for; matrix products, arithmetic and copies ran while one was open for 4% of the time, Pallas kernels for 0%

profile of v1, /device:TPU:32, one launch (start us, length us, event | category | flops | bytes accessed | tf_op | source)
XLA Modules:
  0.0 451.4 jit_solution(662666338853992861)
XLA Ops:
  2.6 16.2 %gather_fusion = bf16[128,2,12,1024]{3,1,2,0:T(2,128)(2,1)} fusion(bf16[64,2,12,1024]{3,1,2,0:T(2,128)(2,1)S(1)} %copy-done, s32[1024]{0:T(1024)S(1)} %pad_clamp_fusion.1), kind=kCustom, calls=%fused_computation | custom fusion | bytes 12583424 | tf_op jit(solution)/shard_map/jit(_take)/gather | solution.py:84
  18.8 8.9 %broadcast_select_fusion = bf16[32,4,2,12,1024]{4,2,3,1,0:T(2,128)(2,1)} fusion(bf16[32,4,2,12,1024]{4,2,3,1,0:T(2,128)(2,1)} %bitcast.66, pred[32,4]{1,0:T(8,128)(4,1)S(1)} %copy.113), kind=kLoop, calls=%fused_computation.3 | loop fusion | flops 3145728 | bytes 12583040 | tf_op jit(solution)/shard_map/jit(_take)/select_n | solution.py:84
  27.7 7.6 %all-to-all-start = ((bf16[32,4,2,12,1024]{4,2,3,1,0:T(2,128)(2,1)}), bf16[32,4,2,12,1024]{4,2,3,1,0:T(2,128)(2,1)}, u32[]{:S(2)}, u32[]{:S(2)}) async-start(bf16[32,4,2,12,1024]{4,2,3,1,0:T(2,128)(2,1)} %broadcast_select_fusion), calls=%async_computation | async-start | bytes 12582912 | tf_op jit(solution)/shard_map/all_to_all | solution.py:85
  37.3 3.0 scatter_custom_fusion
  40.3 74.9 %all-to-all-done = bf16[32,4,2,12,1024]{4,2,3,1,0:T(2,128)(2,1)} async-done(((bf16[32,4,2,12,1024]{4,2,3,1,0:T(2,128)(2,1)}), bf16[32,4,2,12,1024]{4,2,3,1,0:T(2,128)(2,1)}, u32[]{:S(2)}, u32[]{:S(2)}) %all-to-all-start) | async-done | bytes 6291488 | tf_op jit(solution)/shard_map/all_to_all | solution.py:85
  115.1 6.4 %copy.114 = bf16[1,4,2,32,12,1024]{5,2,4,3,1,0:T(2,128)(2,1)S(1)} copy(bf16[1,4,2,32,12,1024]{5,2,4,1,3,0:T(2,128)(2,1)} %bitcast.11) | data formatting | bytes 12582912 | tf_op jit(solution)/shard_map/all_to_all | solution.py:85
  121.5 10.3 %fusion.40 = (bf16[1,4,1,384,1024]{4,2,3,1,0:T(2,128)(2,1)S(1)}, bf16[1,4,1,384,1024]{4,2,3,1,0:T(2,128)(2,1)}) fusion(bf16[1,4,2,384,1024]{4,2,3,1,0:T(2,128)(2,1)S(1)} %bitcast.65), kind=kLoop, calls=%fused_computation.71 | loop fusion | bytes 12582912 | tf_op jit(solution)/shard_map/slice | solution.py:86
  134.9 2.9 copy.123
  137.8 8.4 %convolution_convert_fusion.1 = bf16[4,384,1024]{2,1,0:T(8,128)(2,1)} fusion(f32[4,128,1024]{2,1,0:T(8,128)} %copy-done.2, bf16[1,4,1,384,1024]{4,2,3,1,0:T(2,128)(2,1)} %get-tuple-element.34, bf16[4,128,768]{2,1,0:T(8,128)(2,1)} %bitcast.75), kind=kOutput, calls=%fused_computation.12 | convolution fusion | flops 816840704 | bytes 9175040 | tf_op jit(solution)/shard_map/kcs,kcw->ksw/dot_general | solution.py:98
  146.2 2.7 copy.144
  150.8 3.1 pad_maximum_fusion
  153.9 10.5 %copy.124 = bf16[256,4,2,12,128]{4,1,3,2,0:T(4,128)(2,1)} copy(bf16[256,4,2,12,128]{4,0,3,2,1:T(8,128)(2,1)} %bitcast.68) | data formatting | bytes 12582912 | tf_op jit(solution)/shard_map/reshape | solution.py:102
  164.4 20.5 %all-to-all-start.1 = ((bf16[256,4,2,12,128]{4,1,3,2,0:T(4,128)(2,1)}), bf16[256,4,2,12,128]{4,1,3,2,0:T(4,128)(2,1)}, u32[]{:S(2)}, u32[]{:S(2)}) async-start(bf16[256,4,2,12,128]{4,1,3,2,0:T(4,128)(2,1)} %copy.124), calls=%async_computation.1 | async-start | bytes 12582912 | tf_op jit(solution)/shard_map/all_to_all | solution.py:105
  185.4 141.7 %all-to-all-done.1 = bf16[256,4,2,12,128]{4,1,3,2,0:T(4,128)(2,1)} async-done(((bf16[256,4,2,12,128]{4,1,3,2,0:T(4,128)(2,1)}), bf16[256,4,2,12,128]{4,1,3,2,0:T(4,128)(2,1)}, u32[]{:S(2)}, u32[]{:S(2)}) %all-to-all-start.1) | async-done | bytes 6291488 | tf_op jit(solution)/shard_map/all_to_all | solution.py:105
  327.1 8.7 %copy.125 = bf16[256,4,2,12,128]{4,3,2,1,0:T(8,128)(2,1)} copy(bf16[256,4,2,12,128]{4,1,3,2,0:T(4,128)(2,1)} %all-to-all-done.1) | data formatting | bytes 12582912 | tf_op jit(solution)/shard_map/all_to_all | solution.py:105
  335.7 12.1 %reshape.140 = bf16[1024,3072]{1,0:T(8,128)(2,1)} reshape(bf16[256,4,2,12,128]{4,3,2,1,0:T(8,128)(2,1)} %copy.125) | data formatting | bytes 12582912 | tf_op jit(solution)/shard_map/reshape | solution.py:50
  347.8 8.7 %copy.126 = bf16[3072,1024]{1,0:T(8,128)(2,1)} copy(bf16[3072,1024]{0,1:T(8,128)(2,1)} %bitcast.69) | data formatting | bytes 12582912 | tf_op jit(solution)/shard_map/dot_general | solution.py:51
  356.4 6.9 %subtract_convert_fusion = (bf16[64,2,12,128]{3,0,2,1:T(8,128)(2,1)S(1)}, f32[64,2,12,128]{3,0,2,1:T(8,128)}, f32[64,2,12,128]{3,0,2,1:T(8,128)}) fusion(bf16[64,2,12,128]{3,1,2,0:T(2,128)(2,1)S(1)} %constant_dynamic-slice_fusion.1, f32[64,2,12,128]{3,1,2,0:T(2,128)} %param.14, f32[64,2,12,128]{3,1,2,0:T(2,128)} %param.15, ...), kind=kOutput, calls=%fused_computation.32 | convolution fusion | flops 405471232 | bytes 10227712 | tf_op jit(solution)/shard_map/dot_general | solution.py:51
  363.7 3.3 stack.11
  367.0 4.6 %all-to-all-start.2 = ((bf16[8,64,2,12,128]{4,2,3,1,0:T(2,128)(2,1)}), bf16[8,64,2,12,128]{4,2,3,1,0:T(2,128)(2,1)}, u32[]{:S(2)}, u32[]{:S(2)}) async-start(bf16[8,64,2,12,128]{4,2,3,1,0:T(2,128)(2,1)} %stack.11), calls=%async_computation.2 | async-start | bytes 6291456 | tf_op jit(solution)/shard_map/all_to_all | solution.py:114
  371.6 4.9 %convolution_convert_fusion.2 = bf16[4,128,384]{2,1,0:T(8,128)(2,1)S(1)} fusion(bf16[1,4,1,384,1024]{4,2,3,1,0:T(2,128)(2,1)} %get-tuple-element.34, f32[4,128,1024]{2,1,0:T(8,128)} %copy-done.2), kind=kOutput, calls=%fused_computation.21 | convolution fusion | flops 407568384 | bytes 5636096 | tf_op jit(solution)/shard_map/kcw,ksw->kcs/dot_general | solution.py:91
  381.0 2.6 copy.132
  383.6 60.5 %all-to-all-done.2 = bf16[8,64,2,12,128]{4,2,3,1,0:T(2,128)(2,1)} async-done(((bf16[8,64,2,12,128]{4,2,3,1,0:T(2,128)(2,1)}), bf16[8,64,2,12,128]{4,2,3,1,0:T(2,128)(2,1)}, u32[]{:S(2)}, u32[]{:S(2)}) %all-to-all-start.2) | async-done | bytes 3145760 | tf_op jit(solution)/shard_map/all_to_all | solution.py:114
  444.1 7.0 %copy_bitcast_fusion = bf16[64,2,12,1024]{3,1,2,0:T(2,128)(2,1)} fusion(bf16[8,64,2,12,128]{4,2,3,1,0:T(2,128)(2,1)} %all-to-all-done.2), kind=kLoop, calls=%fused_computation.5 | loop fusion | bytes 6291456
  (45 shorter events, 14.1 us)
Async XLA Ops:
  0.6 1.9 copy-start
  27.7 7.6 %copy-start.5 = (s32[256,4]{0,1:T(4,128)S(1)}, s32[256,4]{0,1:T(4,128)}, u32[]{:S(2)}) copy-start(s32[256,4]{0,1:T(4,128)} %param.11) | copy-start | bytes 12292
  27.7 7.8 %copy-start.6 = (s32[256]{0:T(256)S(1)}, s32[256]{0:T(256)}, u32[]{:S(2)}) copy-start(s32[256]{0:T(256)} %param.10) | copy-start | bytes 3076
  27.7 9.6 %copy-start.4 = (bf16[256,384]{1,0:T(8,128)(2,1)S(1)}, bf16[256,384]{1,0:T(8,128)(2,1)}, u32[]{:S(2)}) copy-start(bf16[256,384]{1,0:T(8,128)(2,1)} %param.9) | copy-start | bytes 589828
  27.7 87.4 %all-to-all-start = ((bf16[32,4,2,12,1024]{4,2,3,1,0:T(2,128)(2,1)}), bf16[32,4,2,12,1024]{4,2,3,1,0:T(2,128)(2,1)}, u32[]{:S(2)}, u32[]{:S(2)}) async-start(bf16[32,4,2,12,1024]{4,2,3,1,0:T(2,128)(2,1)} %broadcast_select_fusion), calls=%async_computation | async-start | bytes 12582912 | tf_op jit(solution)/shard_map/all_to_all | solution.py:85
  121.5 10.3 %copy-start.3 = (bf16[512,768]{1,0:T(8,128)(2,1)S(1)}, bf16[512,768]{1,0:T(8,128)(2,1)}, u32[]{:S(2)}) copy-start(bf16[512,768]{1,0:T(8,128)(2,1)} %scatter_custom_fusion) | copy-start | bytes 2359300
  133.0 1.9 copy-start.2
  148.9 1.9 copy-start.1
  164.4 162.6 %all-to-all-start.1 = ((bf16[256,4,2,12,128]{4,1,3,2,0:T(4,128)(2,1)}), bf16[256,4,2,12,128]{4,1,3,2,0:T(4,128)(2,1)}, u32[]{:S(2)}, u32[]{:S(2)}) async-start(bf16[256,4,2,12,128]{4,1,3,2,0:T(4,128)(2,1)} %copy.124), calls=%async_computation.1 | async-start | bytes 12582912 | tf_op jit(solution)/shard_map/all_to_all | solution.py:105
  367.0 77.1 %all-to-all-start.2 = ((bf16[8,64,2,12,128]{4,2,3,1,0:T(2,128)(2,1)}), bf16[8,64,2,12,128]{4,2,3,1,0:T(2,128)(2,1)}, u32[]{:S(2)}, u32[]{:S(2)}) async-start(bf16[8,64,2,12,128]{4,2,3,1,0:T(2,128)(2,1)} %stack.11), calls=%async_computation.2 | async-start | bytes 6291456 | tf_op jit(solution)/shard_map/all_to_all | solution.py:114
